TPU v7x, 512 devices: a whole 4x8x8 slice. The times are simulated.
512 devices in a mesh: row: 32 (over y_hi, z, core), col: 16 (over y_lo, x).
Axes of the slice: x: 4, y: 8 (y_hi: 2, y_lo: 4; y = y_hi * 4 + y_lo), z: 8, core: 2. Of those that a mesh axis runs over, the one named last changes fastest.
Arguments:
- stress: float32 [256, 16384], P('col', 'row'), may hold values from -2.5 to 2.5
- state: float32 [256, 8192], P('col', 'row'), may hold values from 0 to 1
- load_rate: int32 [256, 16384], P('col', 'row'), may hold values from 0 to 2047
- a_param: float32 [8192], P('row'), may hold values from 1 to 2
- b_param: float32 [8192], P('row'), may hold values from 0.25 to 1
- near_band: bfloat16 [16384, 768], P('row'), may hold values from -0.21875 to 0.21875
- u_far: bfloat16 [64, 64, 32, 256], P('row', 'col'), may hold values from -0.1875 to 0.1875
- v_far: bfloat16 [64, 64, 32, 256], P('row', 'col'), may hold values from -0.375 to 0.375
- ranks: int32 [64, 64], P('row', 'col'), may hold values from 1 to 32, as said below
Outputs:
- new_stress: float32 [256, 16384], P('col', 'row')
- new_state: float32 [256, 8192], P('col', 'row')
Inputs may be any that keep to these rules, and one draw needn't show every extreme that they name: ranks of blocks with |I - J| <= 1 are not used; blocks with |I - J| = 2 have rank 32.
All inputs are finite; a program needn't handle non-finite values.
Results may differ from a plain program's by a relative error of at most 0.0021.
Values may be sent and summed in bfloat16 or wider, within the bound.
No kernel may reach another device: no remote copies, remote signals or barrier semaphores. Data moves between devices by JAX's collectives and lax.ppermute only.
A program may use at most 64 MiB of HBM per device.

v0:
```python
import jax
import jax.numpy as jnp
from jax import lax
from jax.sharding import PartitionSpec as P

B = 128
HSTEP = 0.2
RATE_UNIT = 1.0 / 1024.0


def local(stress, state, load_rate, a_param, b_param, near_band, u_far, v_far, ranks):
    rows = lax.axis_size("row")
    row_index = lax.axis_index("row")
    col_index = lax.axis_index("col")
    block_rows, block_cols, slots, dofs = u_far.shape
    members = stress.shape[0]
    blocks = rows * block_rows
    global_rows = row_index * block_rows + jnp.arange(block_rows, dtype=jnp.int32)
    global_cols = col_index * block_cols + jnp.arange(block_cols, dtype=jnp.int32)
    distant = jnp.abs(global_rows[:, None] - global_cols[None, :]) >= 2
    active = (jnp.arange(slots, dtype=jnp.int32)[None, None, :] < ranks[:, :, None]) & distant[
        :, :, None
    ]
    v_own = jnp.where(active[..., None], v_far, 0).astype(v_far.dtype)
    v_all = lax.all_gather(jnp.swapaxes(v_own, 0, 1), "col", axis=0, tiled=True)
    u_all = lax.all_gather(jnp.swapaxes(u_far, 0, 1), "col", axis=0, tiled=True)

    def to_blocks(value):
        return jnp.swapaxes(value.reshape(members, block_rows, -1), 0, 1)

    def from_blocks(value):
        return jnp.swapaxes(value, 0, 1).reshape(members, -1)

    plate = to_blocks(load_rate.astype(jnp.float32) * RATE_UNIT)
    stress_start, state_start = (to_blocks(stress), to_blocks(state))
    direct = a_param.reshape(block_rows, 1, B)
    evolve = b_param.reshape(block_rows, 1, B)
    band = near_band.reshape(block_rows, dofs, 3, dofs)

    def tendency(stress_now, state_now):
        decay = jnp.exp(-state_now)
        rate_a = 2.0 * decay * jnp.sinh(stress_now[..., :B] / direct)
        rate_b = 2.0 * decay * jnp.sinh(stress_now[..., B:] / direct)
        drift = evolve * (decay - jnp.sqrt(rate_a * rate_a + rate_b * rate_b))
        excess = (jnp.concatenate([rate_a, rate_b], axis=2) - plate).astype(jnp.bfloat16)
        copies = jnp.broadcast_to(excess[None], (rows,) + excess.shape)
        grid = lax.all_to_all(copies, "row", 0, 0).reshape(blocks, members, dofs)
        weights = jnp.einsum("jmd,jird->jmir", grid, v_all, preferred_element_type=jnp.float32)
        weights = weights.astype(jnp.bfloat16)
        total = jnp.einsum("jmir,jird->imd", weights, u_all, preferred_element_type=jnp.float32)
        window = []
        for offset in range(-1, block_rows + 1):
            at = row_index * block_rows + offset
            block = lax.dynamic_index_in_dim(grid, jnp.clip(at, 0, blocks - 1), 0, keepdims=False)
            window.append(jnp.where((at >= 0) & (at < blocks), block, 0).astype(block.dtype))
        windows = jnp.stack([jnp.stack(window[i : i + 3]) for i in range(block_rows)])
        total = total + jnp.einsum(
            "ismd,iksd->imk", windows, band, preferred_element_type=jnp.float32
        )
        return (-total, drift)

    rate_one, drift_one = tendency(stress_start, state_start)
    stress_one = stress_start + HSTEP * rate_one
    state_one = state_start + HSTEP * drift_one
    rate_two, drift_two = tendency(stress_one, state_one)
    stress_two = 0.75 * stress_start + 0.25 * (stress_one + HSTEP * rate_two)
    state_two = 0.75 * state_start + 0.25 * (state_one + HSTEP * drift_two)
    rate_three, drift_three = tendency(stress_two, state_two)
    new_stress = stress_start / 3.0 + 2.0 / 3.0 * (stress_two + HSTEP * rate_three)
    new_state = state_start / 3.0 + 2.0 / 3.0 * (state_two + HSTEP * drift_three)
    return (from_blocks(new_stress), from_blocks(new_state))


def solution(mesh):
    return jax.shard_map(
        local,
        mesh=mesh,
        in_specs=(
            P("col", "row"),
            P("col", "row"),
            P("col", "row"),
            P("row"),
            P("row"),
            P("row", None),
            P("row", "col", None, None),
            P("row", "col", None, None),
            P("row", "col"),
        ),
        out_specs=(P("col", "row"), P("col", "row")),
        check_vma=False,
    )
```

profile of v0, /device:TPU:8, one launch (start us, length us, event | category | flops | bytes accessed | tf_op | source)
XLA Modules:
  0.0 266.0 jit_solution(15811500693297151694)
XLA Ops:
  7.2 0.0 copy-start
  7.2 0.0 copy-start.3
  7.2 0.0 all-gather.3.cloned.1.call-start
  7.3 0.8 copy.54
  8.1 0.1 abs_compare_fusion.6
  8.2 0.1 compare_and_fusion
  8.2 1.7 fusion.23
  9.9 0.0 all-gather.3.cloned.1.call-update
  9.9 0.0 all-gather.5.cloned.1.call-start
  10.0 1.6 copy.106
  11.6 0.0 all-gather.5.cloned.1.call-update
  11.6 0.8 copy.107
  12.3 0.8 convert_multiply_fusion
  13.1 0.0 copy-done
  13.1 0.8 fusion.62
  13.9 0.9 broadcast_in_dim.51
  14.7 0.0 copy-start.4
  14.7 15.2 %all-to-all-start = ((bf16[32,2,16,256]{3,2,1,0:T(8,128)(2,1)}), bf16[32,2,16,256]{3,2,1,0:T(8,128)(2,1)S(1)}, u32[]{:S(2)}, u32[]{:S(2)}) async-start(bf16[32,2,16,256]{3,2,1,0:T(8,128)(2,1)} %broadcast_in_dim.51), calls=%async_computation | async-start | bytes 1048576 | tf_op jit(solution)/shard_map/all_to_all | solution.py:47
  30.0 0.0 copy-done.3
  30.0 0.4 reshape.98
  30.3 0.0 copy-start.2
  30.4 25.7 %all-to-all-done = bf16[32,2,16,256]{3,2,1,0:T(8,128)(2,1)S(1)} async-done(((bf16[32,2,16,256]{3,2,1,0:T(8,128)(2,1)}), bf16[32,2,16,256]{3,2,1,0:T(8,128)(2,1)S(1)}, u32[]{:S(2)}, u32[]{:S(2)}) %all-to-all-start) | async-done | bytes 524320 | tf_op jit(solution)/shard_map/all_to_all | solution.py:47
  56.1 0.3 convolution_bitcast_fusion.2
  56.4 40.5 %all-gather.3.cloned.1.call-done = bf16[64,2,32,256]{3,2,1,0:T(8,128)(2,1)} async-done(((bf16[4,2,32,256]{3,2,1,0:T(8,128)(2,1)}), bf16[64,2,32,256]{3,2,1,0:T(8,128)(2,1)}) %all-gather.3.cloned.1.call-update) | async-done | bytes 2097168 | tf_op jit(solution)/shard_map/all_gather | solution.py:25
  97.0 85.0 %all-gather.5.cloned.1.call-done = bf16[64,2,32,256]{3,2,1,0:T(8,128)(2,1)} async-done(((bf16[4,2,32,256]{3,2,1,0:T(8,128)(2,1)}), bf16[64,2,32,256]{3,2,1,0:T(8,128)(2,1)}) %all-gather.5.cloned.1.call-update) | async-done | bytes 2097168 | tf_op jit(solution)/shard_map/all_gather | solution.py:26
  182.0 0.0 copy-done.2
  182.0 0.0 copy-done.4
  182.0 0.0 copy-start.5
  182.1 0.0 copy-start.6
  182.1 4.0 %fusion.73 = (f32[2,16,256]{2,1,0:T(8,128)S(1)}, f32[2,16,256]{2,1,0:T(8,128)S(1)}) fusion(f32[2,2,8,256]{3,2,1,0:T(8,128)S(1)} %bitcast.238, f32[2,16,256]{2,1,0:T(8,128)S(1)} %convolution_bitcast_fusion.2, bf16[64,2,32,256]{3,2,1,0:T(8,128)(2,1)} %all-gather.5.cloned.1.call-done, bf16[64,16,256,1]{2,1,3,0:T(8,128)(2,1)S(1)} %bitcast.232, ...), kind=kOutput, calls=%fused_computation.132 | convolution fusion | flops 67207168 | bytes 4849664 | tf_op jit(solution)/shard_map/jmir,jird->imd/dot_general | solution.py:50
  186.1 0.0 copy-start.1
  186.1 0.0 copy-done.5
  186.1 0.0 copy-done.6
  186.1 0.1 fusion.65
  186.2 0.1 broadcast_in_dim.55
  186.3 34.7 %all_to_all.15 = bf16[32,2,16,256]{3,2,1,0:T(8,128)(2,1)S(1)} all-to-all(bf16[32,2,16,256]{3,2,1,0:T(8,128)(2,1)S(1)} %broadcast_in_dim.55), channel_id=1, replica_groups=mesh['row'=32,'col'=16] {'row'}, dimensions={0} | all-to-all | bytes 1048576 | tf_op jit(solution)/shard_map/all_to_all | solution.py:47
  221.0 1.5 convolution_bitcast_fusion.1
  222.6 0.0 copy-done.1
  222.6 3.4 %multiply_add_fusion = (f32[2,16,256]{2,1,0:T(8,128)S(1)}, f32[2,16,256]{2,1,0:T(8,128)S(1)}) fusion(f32[2,2,8,256]{3,2,1,0:T(8,128)S(1)} %bitcast.239, f32[2,16,256]{2,1,0:T(8,128)S(1)} %get-tuple-element.30, f32[2,16,256]{2,1,0:T(8,128)S(1)} %convolution_bitcast_fusion.1, bf16[64,2,32,256]{3,2,1,0:T(8,128)(2,1)} %all-gather.5.cloned.1.call-done, ...), kind=kOutput, calls=%fused_computation.55 | convolution fusion | flops 67239936 | bytes 4882432 | tf_op jit(solution)/shard_map/jmir,jird->imd/dot_general | solution.py:50
  226.0 0.1 fusion.67
  226.1 0.9 broadcast_in_dim.56
  226.9 3.9 %all-to-all-start.2 = ((bf16[32,2,16,256]{3,2,1,0:T(8,128)(2,1)}), bf16[32,2,16,256]{3,2,1,0:T(8,128)(2,1)S(1)}, u32[]{:S(2)}, u32[]{:S(2)}) async-start(bf16[32,2,16,256]{3,2,1,0:T(8,128)(2,1)} %broadcast_in_dim.56), calls=%async_computation.2 | async-start | bytes 1048576 | tf_op jit(solution)/shard_map/all_to_all | solution.py:47
  230.8 0.6 copy.108
  231.4 22.1 %all-to-all-done.2 = bf16[32,2,16,256]{3,2,1,0:T(8,128)(2,1)S(1)} async-done(((bf16[32,2,16,256]{3,2,1,0:T(8,128)(2,1)}), bf16[32,2,16,256]{3,2,1,0:T(8,128)(2,1)S(1)}, u32[]{:S(2)}, u32[]{:S(2)}) %all-to-all-start.2) | async-done | bytes 524320 | tf_op jit(solution)/shard_map/all_to_all | solution.py:47
  253.6 1.5 convolution_bitcast_fusion
  255.1 3.4 %fusion.11 = f32[2,2,8,256]{3,2,1,0:T(8,128)S(1)} fusion(f32[2,16,256]{2,1,0:T(8,128)S(1)} %convolution_bitcast_fusion, bf16[64,2,32,256]{3,2,1,0:T(8,128)(2,1)} %all-gather.5.cloned.1.call-done, bf16[64,16,256,1]{2,1,3,0:T(8,128)(2,1)S(1)} %bitcast.234, bf16[64,2,32,256]{3,2,1,0:T(8,128)(2,1)S(1)} %copy-done.1, f32[2,16,256]{2,1,0:T(8,128)S(1)} %get-tuple-element.32, ...), kind=kOutput, calls=%fused_computation.14 | convolution fusion | flops 67272704 | bytes 4882432 | tf_op jit(solution)/shard_map/jmir,jird->imd/dot_general | solution.py:50
  258.5 0.6 copy.75
  (11 shorter events, 0.1 us)
Async XLA Ops:
  7.2 5.9 %copy-start = (f32[16,256]{1,0:T(8,128)S(1)}, f32[16,256]{1,0:T(8,128)}, u32[]{:S(2)}) copy-start(f32[16,256]{1,0:T(8,128)} %param.10) | copy-start | bytes 49156
  7.2 22.8 %copy-start.3 = (bf16[512,768]{1,0:T(8,128)(2,1)S(1)}, bf16[512,768]{1,0:T(8,128)(2,1)}, u32[]{:S(2)}) copy-start(bf16[512,768]{1,0:T(8,128)(2,1)} %param.14) | copy-start | bytes 2359300
  7.2 89.8 %all-gather.3.cloned.1.call-start = ((), (), s32[]{:S(2)}) async-start(), calls=%async_computation.3 | async-start | bytes 2228224 | tf_op jit(solution)/shard_map/all_gather | solution.py:25
  9.9 172.1 %all-gather.5.cloned.1.call-start = ((), (), s32[]{:S(2)}) async-start(), calls=%async_computation.4 | async-start | bytes 2228224 | tf_op jit(solution)/shard_map/all_gather | solution.py:26
  14.7 167.3 %copy-start.4 = (f32[16,512]{1,0:T(8,128)S(1)}, f32[16,512]{1,0:T(8,128)}, u32[]{:S(2)}) copy-start(f32[16,512]{1,0:T(8,128)} %param.9) | copy-start | bytes 98308
  14.7 41.4 %all-to-all-start = ((bf16[32,2,16,256]{3,2,1,0:T(8,128)(2,1)}), bf16[32,2,16,256]{3,2,1,0:T(8,128)(2,1)S(1)}, u32[]{:S(2)}, u32[]{:S(2)}) async-start(bf16[32,2,16,256]{3,2,1,0:T(8,128)(2,1)} %broadcast_in_dim.51), calls=%async_computation | async-start | bytes 1048576 | tf_op jit(solution)/shard_map/all_to_all | solution.py:47
  30.3 151.7 %copy-start.2 = (bf16[2,256,3,256]{3,2,1,0:T(4,128)(2,1)}, bf16[2,256,3,256]{3,2,1,0:T(4,128)(2,1)S(1)}, u32[]{:S(2)}) copy-start(bf16[2,256,3,256]{3,2,1,0:T(4,128)(2,1)S(1)} %reshape.98) | copy-start | bytes 2359300
  182.0 4.1 %copy-start.5 = (f32[256]{0:T(256)S(1)}, f32[256]{0:T(256)}, u32[]{:S(2)}) copy-start(f32[256]{0:T(256)} %param.13) | copy-start | bytes 3076
  182.1 4.1 %copy-start.6 = (f32[256]{0:T(256)S(1)}, f32[256]{0:T(256)}, u32[]{:S(2)}) copy-start(f32[256]{0:T(256)} %param.12) | copy-start | bytes 3076
  186.1 36.5 %copy-start.1 = (bf16[64,2,32,256]{3,2,1,0:T(8,128)(2,1)S(1)}, bf16[64,2,32,256]{3,2,1,0:T(8,128)(2,1)}, u32[]{:S(2)}) copy-start(bf16[64,2,32,256]{3,2,1,0:T(8,128)(2,1)} %all-gather.3.cloned.1.call-done) | copy-start | bytes 6291460
  226.9 26.6 %all-to-all-start.2 = ((bf16[32,2,16,256]{3,2,1,0:T(8,128)(2,1)}), bf16[32,2,16,256]{3,2,1,0:T(8,128)(2,1)S(1)}, u32[]{:S(2)}, u32[]{:S(2)}) async-start(bf16[32,2,16,256]{3,2,1,0:T(8,128)(2,1)} %broadcast_in_dim.56), calls=%async_computation.2 | async-start | bytes 1048576 | tf_op jit(solution)/shard_map/all_to_all | solution.py:47
Sparse Core Ops, SparseCore 0:
  10.1 86.8 all-gather.2
  99.1 82.9 all-gather.4
where the time goes:
time: 267 us; the launch traced here: 266 us
  waiting for transfers between devices  173 us (65%)
  blocking collectives  34.7 us (13%)
  starting transfers between devices  19.2 us (7%)
  matrix products  14.2 us (5%)
  between operations  14.2 us (5%)
  local copies, waits for them, and re-layouts  6.56 us (2%)
  other arithmetic  3.55 us (1%)
    all_gather x1, waiting for transfers between devices, local(): u_all = lax.all_gather(jnp.swapaxes(u_far, 0, 1), 'col', axis=0, tiled=True)  85 us
    all_to_all x2, waiting for transfers between devices, tendency(): grid = lax.all_to_all(copies, 'row', 0, 0).reshape(blocks, members, dofs)  47.9 us
    all_gather x1, waiting for transfers between devices, local(): v_all = lax.all_gather(jnp.swapaxes(v_own, 0, 1), 'col', axis=0, tiled=True)  40.5 us
    all_to_all x1, blocking collectives, tendency(): grid = lax.all_to_all(copies, 'row', 0, 0).reshape(blocks, members, dofs)  34.7 us
    all_to_all x2, starting transfers between devices, tendency(): grid = lax.all_to_all(copies, 'row', 0, 0).reshape(blocks, members, dofs)  19.1 us
    dot_general x3, matrix products, tendency(): jnp.einsum('jmir,jird->imd', weights, u_all, preferred_element_type=jnp.f...  10.8 us
  transfers between devices with their start and end apart: 4, of which 4 were waited for; matrix products, arithmetic and copies ran while one was open for 2% of the time, Pallas kernels for 0%

commit v1 on v0

--- a/solution.py
+++ b/solution.py
@@ -22,7 +22,10 @@
         :, :, None
     ]
     v_own = jnp.where(active[..., None], v_far, 0).astype(v_far.dtype)
-    v_all = lax.all_gather(jnp.swapaxes(v_own, 0, 1), "col", axis=0, tiled=True)
+    v_all = jnp.concatenate(
+        lax.all_to_all(jnp.stack([jnp.swapaxes(v_own, 0, 1)] * lax.axis_size("col")), "col", 0, 0),
+        axis=0,
+    )
     u_all = lax.all_gather(jnp.swapaxes(u_far, 0, 1), "col", axis=0, tiled=True)
 
     def to_blocks(value):

time: 267 us -> 218 us (0.82)
  the two profiles are of different devices: /device:TPU:8 before, /device:TPU:10 now
where the time goes in v1:
time: 218 us; the launch traced here: 217 us
  waiting for transfers between devices  120 us (55%)
  blocking collectives  32.9 us (15%)
  starting transfers between devices  25 us (11%)
  matrix products  14.8 us (7%)
  between operations  14.2 us (7%)
  local copies, waits for them, and re-layouts  7.26 us (3%)
  other arithmetic  3.57 us (2%)
    all_to_all x1, waiting for transfers between devices, local(): lax.all_to_all(jnp.stack([jnp.swapaxes(v_own, 0, 1)] * lax.axis_size('col...  53.6 us
    all_to_all x2, waiting for transfers between devices, tendency(): grid = lax.all_to_all(copies, 'row', 0, 0).reshape(blocks, members, dofs)  42.5 us
    all_to_all x1, blocking collectives, tendency(): grid = lax.all_to_all(copies, 'row', 0, 0).reshape(blocks, members, dofs)  32.9 us
    all_gather x1, waiting for transfers between devices, local(): u_all = lax.all_gather(jnp.swapaxes(u_far, 0, 1), 'col', axis=0, tiled=True)  23 us
    all_to_all x2, starting transfers between devices, tendency(): grid = lax.all_to_all(copies, 'row', 0, 0).reshape(blocks, members, dofs)  19 us
    dot_general x3, matrix products, tendency(): jnp.einsum('jmir,jird->imd', weights, u_all, preferred_element_type=jnp.f...  10.2 us
    all_to_all x1, starting transfers between devices, local(): lax.all_to_all(jnp.stack([jnp.swapaxes(v_own, 0, 1)] * lax.axis_size('col...  6.04 us
    dot_general x3, matrix products, tendency(): jnp.einsum('ismd,iksd->imk', windows, band, preferred_element_type=jnp.fl...  4.6 us
  transfers between devices with their start and end apart: 4, of which 4 were waited for; matrix products, arithmetic and copies ran while one was open for 3% of the time, Pallas kernels for 0%

profile of v1, /device:TPU:10, one launch (start us, length us, event | category | flops | bytes accessed | tf_op | source)
XLA Modules:
  0.0 217.4 jit_solution(14862351182916088303)
XLA Ops:
  7.2 0.0 copy-start
  7.2 0.0 copy-start.3
  7.2 0.8 copy.96
  8.0 0.8 convert_multiply_fusion
  8.8 0.0 copy-done
  8.8 0.8 fusion.61
  9.5 0.9 broadcast_in_dim.51
  10.4 15.1 %all-to-all-start = ((bf16[32,2,16,256]{3,2,1,0:T(8,128)(2,1)}), bf16[32,2,16,256]{3,2,1,0:T(8,128)(2,1)S(1)}, u32[]{:S(2)}, u32[]{:S(2)}) async-start(bf16[32,2,16,256]{3,2,1,0:T(8,128)(2,1)} %broadcast_in_dim.51), calls=%async_computation | async-start | bytes 1048576 | tf_op jit(solution)/shard_map/all_to_all | solution.py:50
  25.5 0.1 abs_compare_fusion.6
  25.6 0.8 fusion.69
  26.3 1.0 select_bitcast_fusion
  27.4 0.0 copy-done.3
  27.4 0.7 copy.95
  28.0 20.2 %all-to-all-done = bf16[32,2,16,256]{3,2,1,0:T(8,128)(2,1)S(1)} async-done(((bf16[32,2,16,256]{3,2,1,0:T(8,128)(2,1)}), bf16[32,2,16,256]{3,2,1,0:T(8,128)(2,1)S(1)}, u32[]{:S(2)}, u32[]{:S(2)}) %all-to-all-start) | async-done | bytes 524320 | tf_op jit(solution)/shard_map/all_to_all | solution.py:50
  48.3 1.6 stack.32
  49.8 0.0 copy-start.1
  49.8 6.0 %all-to-all-start.1 = ((bf16[16,4,2,32,256]{4,3,2,1,0:T(8,128)(2,1)}), bf16[16,4,2,32,256]{4,3,2,1,0:T(8,128)(2,1)S(1)}, u32[]{:S(2)}, u32[]{:S(2)}) async-start(bf16[16,4,2,32,256]{4,3,2,1,0:T(8,128)(2,1)} %stack.32), calls=%async_computation.1 | async-start | bytes 4194304 | tf_op jit(solution)/shard_map/all_to_all | solution.py:26
  55.9 0.0 copy-start.2
  55.9 0.0 all-gather.2.cloned.1.call-start
  55.9 0.7 all-gather.2.cloned.1.call-update
  56.6 0.0 copy-done.1
  56.6 1.2 reshape.104
  57.9 1.5 convolution_bitcast_fusion.2
  59.4 53.6 %all-to-all-done.1 = bf16[16,4,2,32,256]{4,3,2,1,0:T(8,128)(2,1)S(1)} async-done(((bf16[16,4,2,32,256]{4,3,2,1,0:T(8,128)(2,1)}), bf16[16,4,2,32,256]{4,3,2,1,0:T(8,128)(2,1)S(1)}, u32[]{:S(2)}, u32[]{:S(2)}) %all-to-all-start.1) | async-done | bytes 2097184 | tf_op jit(solution)/shard_map/all_to_all | solution.py:26
  112.9 23.0 %all-gather.2.cloned.1.call-done = bf16[64,2,32,256]{3,2,1,0:T(8,128)(2,1)} async-done(((bf16[4,2,32,256]{3,2,1,0:T(8,128)(2,1)}), bf16[64,2,32,256]{3,2,1,0:T(8,128)(2,1)}) %all-gather.2.cloned.1.call-update) | async-done | bytes 2097168 | tf_op jit(solution)/shard_map/all_gather | solution.py:29
  135.9 0.0 copy-done.2
  135.9 0.0 copy-start.4
  135.9 0.0 copy-start.5
  135.9 3.4 %fusion.73 = (f32[2,16,256]{2,1,0:T(8,128)S(1)}, f32[2,16,256]{2,1,0:T(8,128)S(1)}) fusion(f32[2,2,8,256]{3,2,1,0:T(8,128)S(1)} %bitcast.242, f32[2,16,256]{2,1,0:T(8,128)S(1)} %convolution_bitcast_fusion.2, bf16[64,2,32,256]{3,2,1,0:T(8,128)(2,1)} %all-gather.2.cloned.1.call-done, bf16[64,16,256,1]{2,1,3,0:T(8,128)(2,1)S(1)} %bitcast.236, ...), kind=kOutput, calls=%fused_computation.132 | convolution fusion | flops 67207168 | bytes 4849664 | tf_op jit(solution)/shard_map/jmir,jird->imd/dot_general | solution.py:53
  139.3 0.0 copy-done.4
  139.3 0.0 copy-done.5
  139.3 0.1 fusion.64
  139.4 0.1 broadcast_in_dim.55
  139.5 32.9 %all_to_all.20 = bf16[32,2,16,256]{3,2,1,0:T(8,128)(2,1)S(1)} all-to-all(bf16[32,2,16,256]{3,2,1,0:T(8,128)(2,1)S(1)} %broadcast_in_dim.55), channel_id=1, replica_groups=mesh['row'=32,'col'=16] {'row'}, dimensions={0} | all-to-all | bytes 1048576 | tf_op jit(solution)/shard_map/all_to_all | solution.py:50
  172.4 1.5 convolution_bitcast_fusion.1
  173.9 3.4 %multiply_add_fusion = (f32[2,16,256]{2,1,0:T(8,128)S(1)}, f32[2,16,256]{2,1,0:T(8,128)S(1)}) fusion(f32[2,2,8,256]{3,2,1,0:T(8,128)S(1)} %bitcast.243, f32[2,16,256]{2,1,0:T(8,128)S(1)} %get-tuple-element.30, f32[2,16,256]{2,1,0:T(8,128)S(1)} %convolution_bitcast_fusion.1, bf16[64,2,32,256]{3,2,1,0:T(8,128)(2,1)} %all-gather.2.cloned.1.call-done, ...), kind=kOutput, calls=%fused_computation.54 | convolution fusion | flops 67239936 | bytes 4882432 | tf_op jit(solution)/shard_map/jmir,jird->imd/dot_general | solution.py:53
  177.3 0.1 fusion.66
  177.4 0.9 broadcast_in_dim.56
  178.3 3.9 %all-to-all-start.3 = ((bf16[32,2,16,256]{3,2,1,0:T(8,128)(2,1)}), bf16[32,2,16,256]{3,2,1,0:T(8,128)(2,1)S(1)}, u32[]{:S(2)}, u32[]{:S(2)}) async-start(bf16[32,2,16,256]{3,2,1,0:T(8,128)(2,1)} %broadcast_in_dim.56), calls=%async_computation.3 | async-start | bytes 1048576 | tf_op jit(solution)/shard_map/all_to_all | solution.py:50
  182.2 0.6 copy.97
  182.8 22.2 %all-to-all-done.3 = bf16[32,2,16,256]{3,2,1,0:T(8,128)(2,1)S(1)} async-done(((bf16[32,2,16,256]{3,2,1,0:T(8,128)(2,1)}), bf16[32,2,16,256]{3,2,1,0:T(8,128)(2,1)S(1)}, u32[]{:S(2)}, u32[]{:S(2)}) %all-to-all-start.3) | async-done | bytes 524320 | tf_op jit(solution)/shard_map/all_to_all | solution.py:50
  205.0 1.5 convolution_bitcast_fusion
  206.6 3.4 %fusion.11 = f32[2,2,8,256]{3,2,1,0:T(8,128)S(1)} fusion(f32[2,16,256]{2,1,0:T(8,128)S(1)} %convolution_bitcast_fusion, bf16[64,2,32,256]{3,2,1,0:T(8,128)(2,1)} %all-gather.2.cloned.1.call-done, bf16[64,16,256,1]{2,1,3,0:T(8,128)(2,1)S(1)} %bitcast.238, bf16[64,2,32,256]{3,2,1,0:T(8,128)(2,1)S(1)} %bitcast.234, f32[2,16,256]{2,1,0:T(8,128)S(1)} %get-tuple-element.32, ...), kind=kOutput, calls=%fused_computation.14 | convolution fusion | flops 67272704 | bytes 4882432 | tf_op jit(solution)/shard_map/jmir,jird->imd/dot_general | solution.py:53
  210.0 0.6 copy.67
  (12 shorter events, 0.1 us)
Async XLA Ops:
  7.2 1.6 copy-start
  7.2 20.2 %copy-start.3 = (bf16[2,4,32,256]{3,2,1,0:T(8,128)(2,1)S(1)}, bf16[2,4,32,256]{3,2,1,0:T(8,128)(2,1)}, u32[]{:S(2)}) copy-start(bf16[2,4,32,256]{3,2,1,0:T(8,128)(2,1)} %param.15) | copy-start | bytes 393220
  10.4 37.9 %all-to-all-start = ((bf16[32,2,16,256]{3,2,1,0:T(8,128)(2,1)}), bf16[32,2,16,256]{3,2,1,0:T(8,128)(2,1)S(1)}, u32[]{:S(2)}, u32[]{:S(2)}) async-start(bf16[32,2,16,256]{3,2,1,0:T(8,128)(2,1)} %broadcast_in_dim.51), calls=%async_computation | async-start | bytes 1048576 | tf_op jit(solution)/shard_map/all_to_all | solution.py:50
  49.8 6.8 %copy-start.1 = (bf16[512,768]{1,0:T(8,128)(2,1)S(1)}, bf16[512,768]{1,0:T(8,128)(2,1)}, u32[]{:S(2)}) copy-start(bf16[512,768]{1,0:T(8,128)(2,1)} %param.14) | copy-start | bytes 2359300
  49.8 63.1 %all-to-all-start.1 = ((bf16[16,4,2,32,256]{4,3,2,1,0:T(8,128)(2,1)}), bf16[16,4,2,32,256]{4,3,2,1,0:T(8,128)(2,1)S(1)}, u32[]{:S(2)}, u32[]{:S(2)}) async-start(bf16[16,4,2,32,256]{4,3,2,1,0:T(8,128)(2,1)} %stack.32), calls=%async_computation.1 | async-start | bytes 4194304 | tf_op jit(solution)/shard_map/all_to_all | solution.py:26
  55.9 80.0 %copy-start.2 = (f32[16,512]{1,0:T(8,128)S(1)}, f32[16,512]{1,0:T(8,128)}, u32[]{:S(2)}) copy-start(f32[16,512]{1,0:T(8,128)} %param.9) | copy-start | bytes 98308
  55.9 80.0 %all-gather.2.cloned.1.call-start = ((), (), s32[]{:S(2)}) async-start(), calls=%async_computation.4 | async-start | bytes 2228224 | tf_op jit(solution)/shard_map/all_gather | solution.py:29
  135.9 3.4 %copy-start.4 = (f32[256]{0:T(256)S(1)}, f32[256]{0:T(256)}, u32[]{:S(2)}) copy-start(f32[256]{0:T(256)} %param.13) | copy-start | bytes 3076
  135.9 3.4 %copy-start.5 = (f32[256]{0:T(256)S(1)}, f32[256]{0:T(256)}, u32[]{:S(2)}) copy-start(f32[256]{0:T(256)} %param.12) | copy-start | bytes 3076
  178.3 26.7 %all-to-all-start.3 = ((bf16[32,2,16,256]{3,2,1,0:T(8,128)(2,1)}), bf16[32,2,16,256]{3,2,1,0:T(8,128)(2,1)S(1)}, u32[]{:S(2)}, u32[]{:S(2)}) async-start(bf16[32,2,16,256]{3,2,1,0:T(8,128)(2,1)} %broadcast_in_dim.56), calls=%async_computation.3 | async-start | bytes 1048576 | tf_op jit(solution)/shard_map/all_to_all | solution.py:50
Sparse Core Ops, SparseCore 0:
  58.8 77.0 all-gather.1
